TPU v7x, 32 devices: a whole 2x2x4 slice. The times are simulated.
32 devices in a mesh: parts: 2 (over y), clus: 4 (over z), mem: 2 (over x), sub: 2 (over core).
Axes of the slice: x: 2, y: 2, z: 4, core: 2. Of those that a mesh axis runs over, the one named last changes fastest.
Arguments:
- embeddings: bfloat16 [4096, 1024], P(('parts', 'clus', 'mem', 'sub')), parts along dimension 0, as said below
- labels: int32 [4096], P(('parts', 'clus', 'mem', 'sub')), parts along dimension 0, may hold values from 0 to 15, as said below
- member_rank: int32 [4096], P(('parts', 'clus', 'mem', 'sub')), parts along dimension 0, may hold values from 0 to 2047, each once
Outputs:
- nearest: float32 [4096], P(('parts', 'clus', 'mem', 'sub')), parts along dimension 0
There are 2 independent parts, one for each index of `parts`. A program takes and returns all parts, laid end to end along the dimension named above; each array names one. Nothing has to cross between parts.
Inputs may be any that keep to these rules, and one draw needn't show every extreme that they name: `embeddings`: each row has unit length up to rounding. Among the rows of one device, at most 32 have labels in any one group of 2 consecutive clusters (label // 2); on every device some group has exactly 32.
All inputs are finite; a program needn't handle non-finite values.
Results may differ from a plain program's by a relative error of at most 0.0003.
Values may be sent and summed in bfloat16 or wider, within the bound.
A program may use at most 64 MiB of HBM per device.

v0:
```python
import functools
import math

import jax
import jax.numpy as jnp
from jax import lax
from jax.experimental import pallas as pl
from jax.experimental.pallas import tpu as pltpu
from jax.sharding import PartitionSpec as P

CLUS_GROUP = 2
MESH = pl.DeviceIdType.MESH
ROW_TILE = 16
LANES = 128
BYTE = 256
CLASS_STEP = BYTE * BYTE
NO_CAP = 3e38


def flipped(index, mask, size):
    out = 0
    bit = 1
    while bit < size:
        digit = lax.rem(lax.div(index, bit), 2)
        out = out + ((1 - digit) if mask & bit else digit) * bit
        bit *= 2
    return out


def nt_dot(lhs, rhs):
    return lax.dot_general(lhs, rhs, (((1,), (1,)), ((), ())), preferred_element_type=jnp.float32)


def dedup_kernel(
    clus_count,
    mem_count,
    capacity,
    emb_hbm,
    label_hbm,
    rank_hbm,
    out_ref,
    emb,
    label_ref,
    rank_ref,
    caps_own,
    caps_sib,
    send,
    own,
    sib,
    key_out,
    key_in,
    key_own,
    key_sib,
    ret_out,
    ret_in,
    load_sem,
    emb_send,
    emb_recv,
    key_send,
    key_recv,
    fwd_send,
    fwd_recv,
    kf_send,
    kf_recv,
    ret_send,
    ret_recv,
):
    groups = clus_count * mem_count
    rows = emb.shape[0]
    slots = groups * capacity
    tiles = slots // LANES
    per_tile = LANES // capacity
    clus = lax.axis_index("clus")
    mem = lax.axis_index("mem")
    sub = lax.axis_index("sub")
    me = clus * mem_count + mem


    def partner(k):
        return {
            "clus": flipped(clus, k // mem_count, clus_count),
            "mem": flipped(mem, k % mem_count, mem_count),
        }

    sibling = {"sub": 1 - sub}
    load_label = pltpu.make_async_copy(label_hbm, label_ref, load_sem.at[0])
    load_rank = pltpu.make_async_copy(rank_hbm, rank_ref, load_sem.at[1])
    load = pltpu.make_async_copy(emb_hbm, emb, load_sem.at[2])
    load_label.start()
    load.start()
    load_rank.start()
    far_first = list(range(groups - 1, 0, -1))
    barrier = pltpu.get_barrier_semaphore()
    for k in far_first:
        pl.semaphore_signal(barrier, inc=1, device_id=partner(k), device_id_type=MESH)
    pl.semaphore_signal(barrier, inc=1, device_id=sibling, device_id_type=MESH)

    load_label.wait()
    labels = label_ref[...]
    group = lax.div(labels, CLUS_GROUP)
    relative = jnp.bitwise_xor(group, me)
    group_iota = lax.broadcasted_iota(jnp.int32, (groups, rows), 0)
    member = group_iota == relative
    before = lax.broadcasted_iota(jnp.int32, (rows, rows), 0) < lax.broadcasted_iota(
        jnp.int32, (rows, rows), 1
    )
    counts = jnp.dot(
        member.astype(jnp.float32).astype(jnp.bfloat16),
        before.astype(jnp.float32).astype(jnp.bfloat16),
        preferred_element_type=jnp.float32,
    )
    slot = jnp.sum(
        jnp.where(member, counts + (group_iota * capacity).astype(jnp.float32), 0.0),
        axis=0,
        keepdims=True,
    ).astype(jnp.int32)
    place = (
        (lax.broadcasted_iota(jnp.int32, (slots, rows), 0) == slot)
        .astype(jnp.float32)
        .astype(jnp.bfloat16)
    )

    def fill(first, count):
        span = pl.ds(first * capacity, count * capacity)
        send[span, :] = jnp.dot(
            place[first * capacity : (first + count) * capacity],
            emb[...],
            preferred_element_type=jnp.float32,
        ).astype(jnp.bfloat16)

    def send_order(k):
        clus_mask, mem_mask = divmod(k, mem_count)
        near = clus_mask < clus_count // 2
        return near, -clus_mask if near else clus_mask, -mem_mask

    def block(ref, k):
        return ref.at[pl.ds(k * capacity, capacity), :]

    emb_copies, key_copies = {}, {}
    for k in far_first:
        emb_copies[k] = pltpu.make_async_remote_copy(
            src_ref=block(send, k),
            dst_ref=block(own, k),
            send_sem=emb_send.at[k],
            recv_sem=emb_recv.at[k],
            device_id=partner(k),
            device_id_type=MESH,
        )
        key_copies[k] = pltpu.make_async_remote_copy(
            src_ref=key_out.at[k // per_tile],
            dst_ref=key_in.at[k],
            send_sem=key_send.at[k],
            recv_sem=key_recv.at[k],
            device_id=partner(k),
            device_id_type=MESH,
        )
    half = groups // 2
    load_rank.wait()
    ranks = rank_ref[...]
    row_iota = lax.broadcasted_iota(jnp.int32, (8, rows), 0)
    digits = jnp.where(
        row_iota == 0,
        labels - group * CLUS_GROUP + 1,
        jnp.where(
            row_iota == 1,
            lax.div(ranks, BYTE),
            jnp.where(row_iota == 2, lax.rem(ranks, BYTE), 0),
        ),
    )
    placed = nt_dot(digits.astype(jnp.float32).astype(jnp.bfloat16), place)
    keys = placed[0:1] * float(CLASS_STEP) + placed[1:2] * float(BYTE) + placed[2:3]
    for t in range(tiles):
        key_out[t] = keys[:, t * LANES : (t + 1) * LANES]
    load.wait()
    fill(0, groups)
    pl.semaphore_wait(barrier, groups)
    for k in far_first:
        key_copies[k].start()
    for k in sorted(far_first, key=send_order):
        emb_copies[k].start()
    own[pl.ds(0, capacity), :] = send[pl.ds(0, capacity), :]

    forwards = {}
    for k in range(groups):
        forwards[k] = pltpu.make_async_remote_copy(
            src_ref=block(send if k == 0 else own, k),
            dst_ref=block(sib, k),
            send_sem=fwd_send.at[k],
            recv_sem=fwd_recv.at[k],
            device_id=sibling,
            device_id_type=MESH,
        )
    forwards[0].start()
    lane_block = lax.div(lax.broadcasted_iota(jnp.int32, (1, LANES), 1), capacity)
    for k in range(1, groups):
        key_copies[k].wait_recv()
    for t in range(tiles):
        row = jnp.zeros((1, LANES), jnp.float32)
        for k in range(t * per_tile, (t + 1) * per_tile):
            piece = key_out[t] if k == 0 else key_in[k]
            row = jnp.where(lane_block == k % per_tile, piece, row)
        key_own[t] = row
    key_forward = pltpu.make_async_remote_copy(
        src_ref=key_own,
        dst_ref=key_sib,
        send_sem=kf_send,
        recv_sem=kf_recv,
        device_id=sibling,
        device_id_type=MESH,
    )
    key_forward.start()
    row_keys = jnp.concatenate([key_own[t] for t in range(tiles)], axis=1)
    row_base = (
        lax.div(row_keys.astype(jnp.int32), CLASS_STEP) * CLASS_STEP
    ).astype(jnp.float32)
    row_base = jnp.maximum(row_base, 1.0)

    def make_caps(caps, cand_keys):
        for t in range(tiles):
            column = jnp.transpose(jnp.broadcast_to(cand_keys[t], (LANES, LANES)))
            column = jnp.concatenate([column] * tiles, axis=1)
            allowed = (column < row_keys) & (column >= row_base)
            caps[pl.ds(t * LANES, LANES), :] = jnp.where(allowed, NO_CAP, -1.0)

    make_caps(caps_own, key_own)
    key_forward.wait_recv()
    make_caps(caps_sib, key_sib)

    def masked(cands, caps, first, count):
        span = pl.ds(first * capacity, count * capacity)
        scores = jnp.minimum(nt_dot(cands[span, :], own[...]), caps[span, :])
        return jnp.max(scores, axis=0, keepdims=True)

    for k in range(1, groups):
        emb_copies[k].wait_recv()
        forwards[k].start()
    best = jnp.maximum(masked(own, caps_own, 0, groups), -1.0)
    for k in range(groups):
        forwards[k].wait_recv()
    best = jnp.maximum(best, masked(sib, caps_sib, 0, groups))
    for t in range(tiles):
        ret_out[t] = best[:, t * LANES : (t + 1) * LANES]

    returns = {}
    for k in far_first:
        returns[k] = pltpu.make_async_remote_copy(
            src_ref=ret_out.at[k // per_tile],
            dst_ref=ret_in.at[k],
            send_sem=ret_send.at[k],
            recv_sem=ret_recv.at[k],
            device_id=partner(k),
            device_id_type=MESH,
        )
        returns[k].start()
    for k in far_first:
        emb_copies[k].wait_send()
        key_copies[k].wait_send()
    for k in range(groups):
        forwards[k].wait_send()
    key_forward.wait_send()
    for k in range(1, groups):
        returns[k].wait_recv()

    pieces = []
    for t in range(tiles):
        row = jnp.zeros((1, LANES), jnp.float32)
        for k in range(t * per_tile, (t + 1) * per_tile):
            piece = ret_out[t] if k == 0 else ret_in[k]
            row = jnp.where(lane_block == k % per_tile, piece, row)
        pieces.append(row)
    result = jnp.concatenate(pieces, axis=1)
    high = result.astype(jnp.bfloat16).astype(jnp.float32)
    middle = (result - high).astype(jnp.bfloat16).astype(jnp.float32)
    low = result - high - middle
    split_iota = lax.broadcasted_iota(jnp.int32, (8, slots), 0)
    split = jnp.where(
        split_iota == 0,
        high,
        jnp.where(split_iota == 1, middle, jnp.where(split_iota == 2, low, 0.0)),
    ).astype(jnp.bfloat16)
    taken = jnp.dot(split, place, preferred_element_type=jnp.float32)
    out_ref[...] = taken[0:1] + taken[1:2] + taken[2:3]
    for k in far_first:
        returns[k].wait_send()


def kernel_body(clus_count, mem_count, embeddings, labels, member_rank):
    rows, width = embeddings.shape
    groups = clus_count * mem_count
    capacity = 2 * rows // groups
    slots = groups * capacity
    tiles = slots // LANES
    dma = pltpu.SemaphoreType.DMA
    vmem = pl.BlockSpec(memory_space=pltpu.VMEM)
    out = pl.pallas_call(
        functools.partial(dedup_kernel, clus_count, mem_count, capacity),
        out_shape=jax.ShapeDtypeStruct((1, rows), jnp.float32),
        in_specs=[pl.BlockSpec(memory_space=pl.ANY)] * 3,
        out_specs=vmem,
        scratch_shapes=[
            pltpu.VMEM((rows, width), jnp.bfloat16),
            pltpu.VMEM((1, rows), jnp.int32),
            pltpu.VMEM((1, rows), jnp.int32),
            pltpu.VMEM((slots, slots), jnp.float32),
            pltpu.VMEM((slots, slots), jnp.float32),
            pltpu.VMEM((slots, width), jnp.bfloat16),
            pltpu.VMEM((slots, width), jnp.bfloat16),
            pltpu.VMEM((slots, width), jnp.bfloat16),
            pltpu.VMEM((tiles, 1, LANES), jnp.float32),
            pltpu.VMEM((groups, 1, LANES), jnp.float32),
            pltpu.VMEM((tiles, 1, LANES), jnp.float32),
            pltpu.VMEM((tiles, 1, LANES), jnp.float32),
            pltpu.VMEM((tiles, 1, LANES), jnp.float32),
            pltpu.VMEM((groups, 1, LANES), jnp.float32),
            dma((3,)),
            dma((groups,)),
            dma((groups,)),
            dma((groups,)),
            dma((groups,)),
            dma((groups,)),
            dma((groups,)),
            dma,
            dma,
            dma((groups,)),
            dma((groups,)),
        ],
        compiler_params=pltpu.CompilerParams(collective_id=0, has_side_effects=True),
    )(embeddings, labels.reshape(1, rows), member_rank.reshape(1, rows))
    return out.reshape(rows)


def fits_kernel(clus_count, mem_count, sub_count, rows):
    groups = clus_count * mem_count
    capacity = 2 * rows // groups
    return (
        clus_count & (clus_count - 1) == 0
        and mem_count & (mem_count - 1) == 0
        and sub_count == 2
        and groups >= 2
        and rows % LANES == 0
        and capacity % ROW_TILE == 0
        and LANES % capacity == 0
        and rows * groups * sub_count <= CLASS_STEP
    )


def swapped(value, axis, stride):
    mask = 2**stride
    pairs = [(source, source ^ mask) for source in range(lax.axis_size(axis))]
    return lax.ppermute(value, axis, pairs)


def masked_best(row_emb, row_label, row_rank, col_emb, col_label, col_rank, want_columns):
    col_count = col_emb.shape[0]
    block_size = math.gcd(512, col_count)
    block_count = col_count // block_size
    emb_blocks = col_emb.reshape(block_count, block_size, col_emb.shape[1])
    label_blocks = col_label.reshape(block_count, block_size)
    rank_blocks = col_rank.reshape(block_count, block_size)

    def visit_block(running, column_piece):
        piece_emb, piece_label, piece_rank = column_piece
        scores = lax.dot_general(
            row_emb, piece_emb, (((1,), (1,)), ((), ())), preferred_element_type=jnp.float32
        )
        same_cluster = (row_label[:, None] == piece_label[None, :]) & (row_label[:, None] >= 0)
        earlier = piece_rank[None, :] < row_rank[:, None]
        row_best = jnp.max(jnp.where(same_cluster & earlier, scores, jnp.float32(-1.0)), axis=1)
        if want_columns:
            later = same_cluster & jnp.logical_not(earlier)
            col_best = jnp.max(jnp.where(later, scores, jnp.float32(-1.0)), axis=0)
        else:
            col_best = jnp.zeros((0,), jnp.float32)
        return (jnp.maximum(running, row_best), col_best)

    initial = jnp.full((row_emb.shape[0],), -1.0, jnp.float32)
    row_best, col_blocks = lax.scan(visit_block, initial, (emb_blocks, label_blocks, rank_blocks))
    return (row_best, col_blocks.reshape(-1))


def body(embeddings, labels, member_rank):
    row_count = embeddings.shape[0]
    feature_count = embeddings.shape[1]
    clus_count = lax.axis_size("clus")
    mem_count = lax.axis_size("mem")
    group_count = clus_count * mem_count
    capacity = 2 * row_count // group_count
    slot_count = group_count * capacity
    group_of = labels // CLUS_GROUP
    one_hot = (group_of[:, None] == jnp.arange(group_count, dtype=jnp.int32)[None, :]).astype(
        jnp.int32
    )
    running_count = jnp.cumsum(one_hot, axis=0) - 1
    within_group = jnp.sum(one_hot * running_count, axis=1)
    slot_of = group_of * capacity + within_group
    send_emb = jnp.zeros((slot_count, feature_count), jnp.bfloat16).at[slot_of].set(embeddings)
    send_label = jnp.full((slot_count,), -1, jnp.int32).at[slot_of].set(labels)
    send_rank = jnp.zeros((slot_count,), jnp.int32).at[slot_of].set(member_rank)
    received = (
        lax.all_to_all(
            send_emb.reshape(group_count, capacity, feature_count),
            ("clus", "mem"),
            split_axis=0,
            concat_axis=0,
            tiled=True,
        ),
        lax.all_to_all(
            send_label.reshape(group_count, capacity),
            ("clus", "mem"),
            split_axis=0,
            concat_axis=0,
            tiled=True,
        ),
        lax.all_to_all(
            send_rank.reshape(group_count, capacity),
            ("clus", "mem"),
            split_axis=0,
            concat_axis=0,
            tiled=True,
        ),
    )
    own_emb = received[0].reshape(slot_count, feature_count)
    own_label = received[1].reshape(slot_count)
    own_rank = received[2].reshape(slot_count)
    other_emb, other_label, other_rank = swapped((own_emb, own_label, own_rank), "sub", 0)
    diag_best, ignored = masked_best(
        own_emb, own_label, own_rank, own_emb, own_label, own_rank, False
    )
    core_side = lax.axis_index("sub")
    is_zero = core_side == 0
    zero_emb = jnp.where(is_zero, own_emb, other_emb)
    zero_label = jnp.where(is_zero, own_label, other_label)
    zero_rank = jnp.where(is_zero, own_rank, other_rank)
    one_emb = jnp.where(is_zero, other_emb, own_emb)
    one_label = jnp.where(is_zero, other_label, own_label)
    one_rank = jnp.where(is_zero, other_rank, own_rank)
    half_count = slot_count // 2
    offset = core_side * half_count
    part_emb = lax.dynamic_slice_in_dim(zero_emb, offset, half_count, 0)
    part_label = lax.dynamic_slice_in_dim(zero_label, offset, half_count, 0)
    part_rank = lax.dynamic_slice_in_dim(zero_rank, offset, half_count, 0)
    half_best, col_part = masked_best(
        part_emb, part_label, part_rank, one_emb, one_label, one_rank, True
    )
    got_half, got_cols = swapped((half_best, col_part), "sub", 0)
    row_side = jnp.concatenate([half_best, got_half])
    cross_best = jnp.where(is_zero, row_side, jnp.maximum(col_part, got_cols))
    nearest = jnp.maximum(diag_best, cross_best)
    returned = lax.all_to_all(
        nearest.reshape(group_count, capacity),
        ("clus", "mem"),
        split_axis=0,
        concat_axis=0,
        tiled=True,
    )
    return returned.reshape(-1)[slot_of]


def local(embeddings, labels, member_rank):
    rows = embeddings.shape[0]
    clus_count, mem_count, sub_count = (lax.axis_size(a) for a in ("clus", "mem", "sub"))
    if fits_kernel(clus_count, mem_count, sub_count, rows):
        return kernel_body(clus_count, mem_count, embeddings, labels, member_rank)
    return body(embeddings, labels, member_rank)


def solution(mesh):
    placed = (
        P(("parts", "clus", "mem", "sub"), None),
        P(("parts", "clus", "mem", "sub")),
        P(("parts", "clus", "mem", "sub")),
    )
    return jax.shard_map(
        local,
        mesh=mesh,
        in_specs=placed,
        out_specs=P(("parts", "clus", "mem", "sub")),
        check_vma=False,
    )
```

profile of v0, /device:TPU:0, one launch (start us, length us, event | category | flops | bytes accessed | tf_op | source)
XLA Modules:
  0.0 24.8 jit_solution(13506614808256121595)
XLA Ops:
  0.0 23.7 %shard_map.37 = f32[1,128]{1,0:T(1,128)} custom-call(bf16[128,1024]{1,0:T(8,128)(2,1)} %emb_hbm.1, s32[1,128]{1,0:T(1,128)} %bitcast.3, s32[1,128]{1,0:T(1,128)} %bitcast.4), custom_call_target="tpu_custom_call" | custom-call | tf_op jit(solution)/shard_map/pallas_call | solution.py:295
  23.7 0.0 copy-start
  23.7 0.6 %copy-done = f32[1,128]{1,0:T(1,128)S(1)} copy-done((f32[1,128]{1,0:T(1,128)S(1)}, f32[1,128]{1,0:T(1,128)}, u32[]{:S(2)}) %copy-start) | copy-done | bytes 536
  24.3 0.5 %copy.5 = f32[128]{0:T(128)} copy(f32[128]{0:T(128)S(1)} %bitcast.5) | data formatting | bytes 1024
Async XLA Ops:
  23.7 0.6 %copy-start = (f32[1,128]{1,0:T(1,128)S(1)}, f32[1,128]{1,0:T(1,128)}, u32[]{:S(2)}) copy-start(f32[1,128]{1,0:T(1,128)} %shard_map.37) | copy-start | bytes 1540
where the time goes:
time: 25 us; the launch traced here: 24.8 us
  Pallas kernels  23.7 us (95%)
  local copies, waits for them, and re-layouts  1.1 us (4%)
    pallas_call x1, Pallas kernels, kernel_body(): pl.pallas_call(functools.partial(dedup_kernel, clus_count, mem_count, cap...  23.7 us
    unnamed x3, local copies, waits for them, and re-layouts  1.1 us

commit v1 on v0

v1 whole, which is shorter than its diff:
```python
import functools
import math

import jax
import jax.numpy as jnp
from jax import lax
from jax.experimental import pallas as pl
from jax.experimental.pallas import tpu as pltpu
from jax.sharding import PartitionSpec as P

CLUS_GROUP = 2
MESH = pl.DeviceIdType.MESH
LANES = 128
PAIR = 2
PIECES = 4
CLASS_STEP = 65536
EXACT = 2**24


def nt_dot(lhs, rhs):
    return lax.dot_general(lhs, rhs, (((1,), (1,)), ((), ())), preferred_element_type=jnp.float32)


def dedup_kernel(
    emb_hbm,
    label_hbm,
    rank_hbm,
    out_ref,
    side,
    twin,
    far_rows,
    relay,
    key_side,
    key_twin,
    key_far,
    best,
    best_far,
    ret_out,
    ret_in,
    load_sem,
    send_sem,
    recv_sem,
):
    rows, _ = emb_hbm.shape
    chunk = rows // PIECES
    part = lax.axis_index("parts")
    clus = lax.axis_index("clus")
    mem = lax.axis_index("mem")
    sub = lax.axis_index("sub")
    clus_count = lax.axis_size("clus")
    parity = lax.rem(clus, 2)
    along = clus + 1 - 2 * parity
    across = clus_count - 1 - clus
    beyond = clus_count - 1 - along
    is_inner = (clus >= 1) & (clus < clus_count - 1)
    gives = lax.div(clus, 2) != part
    to_along = {"clus": along}
    to_across = {"clus": across}
    to_column = {"mem": 1 - mem}
    to_twin = {"sub": 1 - sub}
    to_part = {"parts": 1 - part}

    used = {}

    def copy(name, src, dst, device):
        slot = used.setdefault(name, len(used))
        return pltpu.make_async_remote_copy(
            src_ref=src,
            dst_ref=dst,
            send_sem=send_sem.at[slot],
            recv_sem=recv_sem.at[slot],
            device_id=device,
            device_id_type=MESH,
        )

    def span(k, count=1):
        return pl.ds(k * chunk, count * chunk)

    def piece(ref, slot, k, count=1):
        return ref.at[slot, span(k, count), :]

    load_label = pltpu.make_async_copy(label_hbm, key_side.at[0, 0], load_sem.at[0])
    load_rank = pltpu.make_async_copy(rank_hbm, key_side.at[0, 1], load_sem.at[1])
    load_rows = pltpu.make_async_copy(emb_hbm, side.at[0], load_sem.at[2])

    half = PIECES // 2
    up = [copy(("up", k), emb_hbm.at[span(k), :], piece(side, 1, k), to_along) for k in range(PIECES)]
    swing = [
        copy(("swing", k), emb_hbm.at[span(k), :], piece(side, 3, k), to_column)
        for k in range(half, PIECES)
    ]
    swing_up = [
        copy(("swing_up", k), piece(side, 3, k), piece(side, 3, k), to_along)
        for k in range(half, PIECES)
    ]
    key_up = [
        copy("label_up", label_hbm, key_side.at[1, 0], to_along),
        copy("rank_up", rank_hbm, key_side.at[1, 1], to_along),
    ]
    wide = [
        copy(("wide", k), emb_hbm.at[span(k), :], piece(side, 2, k), to_column)
        for k in range(PIECES)
    ]
    wide_outer = [
        copy(("wide_outer", k), piece(side, 1, k), piece(side, 3, k), to_column)
        for k in range(half)
    ]
    key_wide = copy("key_wide", key_side.at[pl.ds(0, 2)], key_side.at[pl.ds(2, 2)], to_column)
    pass_own = copy("pass_own", emb_hbm, twin.at[0], to_twin)
    pass_outer = [
        copy(("pass_outer", k), piece(side, 1, k), piece(twin, 1, k), to_twin)
        for k in range(PIECES)
    ]
    key_pass = copy("key_pass", key_side.at[pl.ds(0, 2)], key_twin, to_twin)
    cross_own = [
        copy(("cross_own", k), emb_hbm.at[span(k), :], piece(far_rows, 0, k), to_across)
        for k in range(half, PIECES)
    ]
    cross_outer = [
        copy(("cross_outer", k), piece(side, 1, k), piece(far_rows, 1, k), to_across)
        for k in range(PIECES)
    ]
    key_cross = copy("key_cross", key_side.at[pl.ds(0, 2)], key_far.at[pl.ds(0, 2)], to_across)
    lend = [
        copy(("lend", k), emb_hbm.at[span(k), :], relay.at[span(k), :], to_part)
        for k in range(half)
    ]
    lend_on = [
        copy(
            ("lend_on", k),
            relay.at[span(k), :],
            piece(far_rows, 0, k),
            {"parts": 1 - part, "clus": across},
        )
        for k in range(half)
    ]
    share_own = [
        copy(("share_own", k), piece(far_rows, 0, k), piece(far_rows, 2, k), to_twin)
        for k in range(PIECES)
    ]
    share_outer = [
        copy(("share_outer", k), piece(far_rows, 1, k), piece(far_rows, 3, k), to_twin)
        for k in range(PIECES)
    ]
    key_share = copy("key_share", key_far.at[pl.ds(0, 2)], key_far.at[pl.ds(2, 2)], to_twin)
    back = {
        "outer": copy("back_outer", ret_out.at[1], ret_in.at[0], to_along),
        "inner": copy("back_inner", ret_out.at[2], ret_in.at[1], to_column),
        "outer_wide": copy(
            "back_outer_wide", ret_out.at[3], ret_in.at[1], {"clus": along, "mem": 1 - mem}
        ),
    }
    home = [
        copy("home_0", ret_out.at[4], ret_in.at[2], to_across),
        copy("home_1", ret_out.at[5], ret_in.at[2], {"clus": beyond}),
        copy("home_2", ret_out.at[6], ret_in.at[3], {"clus": across, "sub": 1 - sub}),
        copy("home_3", ret_out.at[7], ret_in.at[3], {"clus": beyond, "sub": 1 - sub}),
    ]

    barrier = pltpu.get_barrier_semaphore()

    def greet(devices):
        for device in devices:
            pl.semaphore_signal(barrier, inc=1, device_id=device, device_id_type=MESH)
        return len(devices)

    def key_of(ref, slot):
        return (ref[slot, 0] * CLASS_STEP + ref[slot, 1]).astype(jnp.float32)

    def cluster(key):
        return jnp.floor(key * (1.0 / CLASS_STEP))

    def column(key_ref, slot):
        return jnp.transpose(jnp.broadcast_to(key_of(key_ref, slot), (LANES, rows)))

    def visit(source, slot, first, count, key_ref, tiles, far_slot=None):
        size = count * chunk
        cand_key = column(key_ref, slot)[first * chunk : first * chunk + size]
        cand_cluster = cluster(cand_key)
        members = side[tiles[0] : tiles[-1] + 1].reshape(len(tiles) * rows, side.shape[2])
        scores = nt_dot(source[slot, span(first, count), :], members)
        reverse = None
        for n, tile in enumerate(tiles):
            score = scores[:, n * rows : (n + 1) * rows]
            member_key = key_of(key_side, tile)
            same = cand_cluster == cluster(member_key)
            earlier = same & (cand_key < member_key)
            top = jnp.max(jnp.where(earlier, score, -1.0), axis=0, keepdims=True)
            best[tile] = jnp.maximum(best[tile], top)
            if far_slot is not None:
                later = jnp.where(same & (cand_key > member_key), score, -1.0)
                reverse = later if reverse is None else jnp.maximum(reverse, later)
        if far_slot is not None:
            part_rows = span(first, count)
            best_far[far_slot, part_rows, :] = jnp.maximum(
                best_far[far_slot, part_rows, :], reverse
            )

    def open_inner(gives_here):
        load_label.start()
        load_rank.start()
        load_rows.start()
        met = greet([to_along, to_across, to_column, to_twin, to_part])
        best[...] = jnp.full(best.shape, -1.0, jnp.float32)
        pl.semaphore_wait(barrier, met)
        if gives_here:
            for c in lend + cross_own:
                c.start()
        for c in wide:
            c.start()
        pass_own.start()
        load_label.wait()
        load_rank.wait()
        for c in key_up:
            c.wait_recv()
        key_pass.start()
        key_wide.start()
        if gives_here:
            key_cross.start()

    def outer_arrived(k, gives_here):
        up[k].wait_recv()
        if gives_here:
            cross_outer[k].start()
        if k < half:
            wide_outer[k].start()
        pass_outer[k].start()

    def settle(copies):
        for c in copies:
            c.wait_recv()

    inner_sent = wide + wide_outer + pass_outer + [pass_own, key_wide, key_pass]

    def result(slots):
        value = ret_in[slots[0]]
        for slot in slots[1:]:
            value = jnp.maximum(value, ret_in[slot])
        return value

    near_tiles = [0, 1, 2]
    last_tile = [3]

    @pl.when(jnp.logical_not(is_inner))
    def _():
        met = greet([to_along, to_column])
        pl.semaphore_wait(barrier, met)
        for c in key_up + up + swing:
            c.start()
        for c, onward in zip(swing, swing_up, strict=True):
            c.wait_recv()
            onward.start()
        back["outer"].wait_recv()
        back["outer_wide"].wait_recv()

        @pl.when(gives)
        def _():
            home[1].wait_recv()
            home[3].wait_recv()
            out_ref[...] = result([0, 1, 2, 3])

        @pl.when(jnp.logical_not(gives))
        def _():
            out_ref[...] = result([0, 1])

        for c in key_up + up + swing + swing_up:
            c.wait_send()

    @pl.when(is_inner & gives)
    def _():
        open_inner(True)
        for k in range(PIECES):
            outer_arrived(k, True)
        load_rows.wait()
        settle([key_wide, key_pass, pass_own] + pass_outer + wide)
        for slot in range(2):
            visit(side, slot, 0, PIECES, key_side, near_tiles)
            visit(twin, slot, 0, PIECES, key_twin, near_tiles)
        for tile in near_tiles[1:]:
            ret_out[tile] = best[tile]
        back["outer"].start()
        back["inner"].start()
        settle(wide_outer + swing_up)
        for slot in range(2):
            visit(side, slot, 0, PIECES, key_side, last_tile)
            visit(twin, slot, 0, PIECES, key_twin, last_tile)
        ret_out[3] = best[3]
        back["outer_wide"].start()
        back["inner"].wait_recv()
        home[0].wait_recv()
        home[2].wait_recv()
        out_ref[...] = jnp.maximum(best[0], result([1, 2, 3]))
        for c in inner_sent + lend + cross_own + cross_outer + [key_cross] + list(back.values()):
            c.wait_send()

    @pl.when(is_inner & jnp.logical_not(gives))
    def _():
        best_far[...] = jnp.full(best_far.shape, -1.0, jnp.float32)
        open_inner(False)
        for k in range(half):
            outer_arrived(k, False)
            lend[k].wait_recv()
            lend_on[k].start()
            cross_own[k].wait_recv()
            share_own[half + k].start()
        outer_arrived(2, False)
        key_cross.wait_recv()
        key_share.start()
        cross_outer[0].wait_recv()
        share_outer[0].start()
        outer_arrived(3, False)
        cross_outer[1].wait_recv()
        share_outer[1].start()
        load_rows.wait()
        settle([key_wide, key_pass, pass_own] + pass_outer + wide)
        for slot in range(2):
            visit(side, slot, 0, PIECES, key_side, near_tiles)
            visit(twin, slot, 0, PIECES, key_twin, near_tiles)
        for k in range(half):
            lend_on[k].wait_recv()
            share_own[k].start()
        cross_outer[2].wait_recv()
        share_outer[2].start()
        key_share.wait_recv()
        visit(far_rows, 0, 0, PIECES, key_far, near_tiles, 0)
        settle(share_own)
        visit(far_rows, 2, 0, PIECES, key_far, near_tiles, 2)
        cross_outer[3].wait_recv()
        share_outer[3].start()
        visit(far_rows, 1, 0, PIECES, key_far, near_tiles, 1)
        settle(wide_outer + swing_up)
        for slot in range(2):
            visit(side, slot, 0, PIECES, key_side, last_tile)
            visit(twin, slot, 0, PIECES, key_twin, last_tile)
        for slot in range(3):
            visit(far_rows, slot, 0, PIECES, key_far, last_tile, slot)
        for slot in range(3):
            ret_out[4 + slot] = jnp.max(jnp.transpose(best_far[slot]), axis=0, keepdims=True)
        for c in home[:3]:
            c.start()
        settle(share_outer)
        visit(far_rows, 3, 0, PIECES, key_far, near_tiles + last_tile, 3)
        for tile in near_tiles[1:] + last_tile:
            ret_out[tile] = best[tile]
        for c in back.values():
            c.start()
        ret_out[7] = jnp.max(jnp.transpose(best_far[3]), axis=0, keepdims=True)
        home[3].start()
        back["inner"].wait_recv()
        out_ref[...] = jnp.maximum(best[0], result([1]))
        for c in inner_sent + lend_on + share_own + share_outer + [key_share] + home + list(back.values()):
            c.wait_send()


COPIES = 64


def kernel_body(embeddings, labels, member_rank):
    rows, width = embeddings.shape
    chunk = rows // PIECES
    dma = pltpu.SemaphoreType.DMA
    kept = embeddings.dtype
    out = pl.pallas_call(
        dedup_kernel,
        out_shape=jax.ShapeDtypeStruct((1, rows), jnp.float32),
        in_specs=[pl.BlockSpec(memory_space=pl.ANY)] * 3,
        out_specs=pl.BlockSpec(memory_space=pltpu.VMEM),
        scratch_shapes=[
            pltpu.VMEM((4, rows, width), kept),
            pltpu.VMEM((2, rows, width), kept),
            pltpu.VMEM((4, rows, width), kept),
            pltpu.VMEM((rows // 2, width), kept),
            pltpu.VMEM((4, 2, 1, rows), jnp.int32),
            pltpu.VMEM((2, 2, 1, rows), jnp.int32),
            pltpu.VMEM((4, 2, 1, rows), jnp.int32),
            pltpu.VMEM((4, 1, rows), jnp.float32),
            pltpu.VMEM((4, rows, rows), jnp.float32),
            pltpu.VMEM((8, 1, rows), jnp.float32),
            pltpu.VMEM((4, 1, rows), jnp.float32),
            dma((3,)),
            dma((COPIES,)),
            dma((COPIES,)),
        ],
        compiler_params=pltpu.CompilerParams(collective_id=0, has_side_effects=True),
    )(embeddings, labels.reshape(1, rows), member_rank.reshape(1, rows))
    return out.reshape(rows)


def fits_kernel(rows):
    parts, clus, mem, sub = (lax.axis_size(a) for a in ("parts", "clus", "mem", "sub"))
    members = rows * clus * mem * sub
    clusters = CLUS_GROUP * clus * mem
    return (
        parts == mem == sub == PAIR
        and clus == 2 * PAIR
        and rows == LANES
        and members <= CLASS_STEP
        and clusters * CLASS_STEP <= EXACT
    )


def swapped(value, axis, stride):
    mask = 2**stride
    pairs = [(source, source ^ mask) for source in range(lax.axis_size(axis))]
    return lax.ppermute(value, axis, pairs)


def masked_best(row_emb, row_label, row_rank, col_emb, col_label, col_rank, want_columns):
    col_count = col_emb.shape[0]
    block_size = math.gcd(512, col_count)
    block_count = col_count // block_size
    emb_blocks = col_emb.reshape(block_count, block_size, col_emb.shape[1])
    label_blocks = col_label.reshape(block_count, block_size)
    rank_blocks = col_rank.reshape(block_count, block_size)

    def visit_block(running, column_piece):
        piece_emb, piece_label, piece_rank = column_piece
        scores = lax.dot_general(
            row_emb, piece_emb, (((1,), (1,)), ((), ())), preferred_element_type=jnp.float32
        )
        same_cluster = (row_label[:, None] == piece_label[None, :]) & (row_label[:, None] >= 0)
        earlier = piece_rank[None, :] < row_rank[:, None]
        row_best = jnp.max(jnp.where(same_cluster & earlier, scores, jnp.float32(-1.0)), axis=1)
        if want_columns:
            later = same_cluster & jnp.logical_not(earlier)
            col_best = jnp.max(jnp.where(later, scores, jnp.float32(-1.0)), axis=0)
        else:
            col_best = jnp.zeros((0,), jnp.float32)
        return (jnp.maximum(running, row_best), col_best)

    initial = jnp.full((row_emb.shape[0],), -1.0, jnp.float32)
    row_best, col_blocks = lax.scan(visit_block, initial, (emb_blocks, label_blocks, rank_blocks))
    return (row_best, col_blocks.reshape(-1))


def body(embeddings, labels, member_rank):
    row_count = embeddings.shape[0]
    feature_count = embeddings.shape[1]
    clus_count = lax.axis_size("clus")
    mem_count = lax.axis_size("mem")
    group_count = clus_count * mem_count
    capacity = 2 * row_count // group_count
    slot_count = group_count * capacity
    group_of = labels // CLUS_GROUP
    one_hot = (group_of[:, None] == jnp.arange(group_count, dtype=jnp.int32)[None, :]).astype(
        jnp.int32
    )
    running_count = jnp.cumsum(one_hot, axis=0) - 1
    within_group = jnp.sum(one_hot * running_count, axis=1)
    slot_of = group_of * capacity + within_group
    send_emb = jnp.zeros((slot_count, feature_count), jnp.bfloat16).at[slot_of].set(embeddings)
    send_label = jnp.full((slot_count,), -1, jnp.int32).at[slot_of].set(labels)
    send_rank = jnp.zeros((slot_count,), jnp.int32).at[slot_of].set(member_rank)
    received = (
        lax.all_to_all(
            send_emb.reshape(group_count, capacity, feature_count),
            ("clus", "mem"),
            split_axis=0,
            concat_axis=0,
            tiled=True,
        ),
        lax.all_to_all(
            send_label.reshape(group_count, capacity),
            ("clus", "mem"),
            split_axis=0,
            concat_axis=0,
            tiled=True,
        ),
        lax.all_to_all(
            send_rank.reshape(group_count, capacity),
            ("clus", "mem"),
            split_axis=0,
            concat_axis=0,
            tiled=True,
        ),
    )
    own_emb = received[0].reshape(slot_count, feature_count)
    own_label = received[1].reshape(slot_count)
    own_rank = received[2].reshape(slot_count)
    other_emb, other_label, other_rank = swapped((own_emb, own_label, own_rank), "sub", 0)
    diag_best, ignored = masked_best(
        own_emb, own_label, own_rank, own_emb, own_label, own_rank, False
    )
    core_side = lax.axis_index("sub")
    is_zero = core_side == 0
    zero_emb = jnp.where(is_zero, own_emb, other_emb)
    zero_label = jnp.where(is_zero, own_label, other_label)
    zero_rank = jnp.where(is_zero, own_rank, other_rank)
    one_emb = jnp.where(is_zero, other_emb, own_emb)
    one_label = jnp.where(is_zero, other_label, own_label)
    one_rank = jnp.where(is_zero, other_rank, own_rank)
    half_count = slot_count // 2
    offset = core_side * half_count
    part_emb = lax.dynamic_slice_in_dim(zero_emb, offset, half_count, 0)
    part_label = lax.dynamic_slice_in_dim(zero_label, offset, half_count, 0)
    part_rank = lax.dynamic_slice_in_dim(zero_rank, offset, half_count, 0)
    half_best, col_part = masked_best(
        part_emb, part_label, part_rank, one_emb, one_label, one_rank, True
    )
    got_half, got_cols = swapped((half_best, col_part), "sub", 0)
    row_side = jnp.concatenate([half_best, got_half])
    cross_best = jnp.where(is_zero, row_side, jnp.maximum(col_part, got_cols))
    nearest = jnp.maximum(diag_best, cross_best)
    returned = lax.all_to_all(
        nearest.reshape(group_count, capacity),
        ("clus", "mem"),
        split_axis=0,
        concat_axis=0,
        tiled=True,
    )
    return returned.reshape(-1)[slot_of]


def local(embeddings, labels, member_rank):
    if fits_kernel(embeddings.shape[0]):
        return kernel_body(embeddings, labels, member_rank)
    return body(embeddings, labels, member_rank)


def solution(mesh):
    placed = (
        P(("parts", "clus", "mem", "sub"), None),
        P(("parts", "clus", "mem", "sub")),
        P(("parts", "clus", "mem", "sub")),
    )
    return jax.shard_map(
        local,
        mesh=mesh,
        in_specs=placed,
        out_specs=P(("parts", "clus", "mem", "sub")),
        check_vma=False,
    )
```

time: 25 us -> 23.9 us (0.956)
  Pallas kernels: 23.7 us -> 22.6 us
    pallas_call x1, Pallas kernels: 23.7 us -> 22.6 us  [kernel_body(): pl.pallas_call(dedup_kernel, out_shape=jax.ShapeDtypeStruct((1, rows), jn...]
where the time goes in v1:
time: 23.9 us; the launch traced here: 23.7 us
  Pallas kernels  22.6 us (95%)
  local copies, waits for them, and re-layouts  1.1 us (5%)
    pallas_call x1, Pallas kernels, kernel_body(): pl.pallas_call(dedup_kernel, out_shape=jax.ShapeDtypeStruct((1, rows), jn...  22.6 us
    unnamed x3, local copies, waits for them, and re-layouts  1.1 us

profile of v1, /device:TPU:0, one launch (start us, length us, event | category | flops | bytes accessed | tf_op | source)
XLA Modules:
  0.0 23.7 jit_solution(16359487283675989844)
XLA Ops:
  0.0 22.6 %shard_map.37 = f32[1,128]{1,0:T(1,128)} custom-call(bf16[128,1024]{1,0:T(8,128)(2,1)} %emb_hbm.1, s32[1,128]{1,0:T(1,128)} %bitcast.3, s32[1,128]{1,0:T(1,128)} %bitcast.4), custom_call_target="tpu_custom_call" | custom-call | tf_op jit(solution)/shard_map/pallas_call | solution.py:363
  22.6 0.0 copy-start
  22.6 0.6 %copy-done = f32[1,128]{1,0:T(1,128)S(1)} copy-done((f32[1,128]{1,0:T(1,128)S(1)}, f32[1,128]{1,0:T(1,128)}, u32[]{:S(2)}) %copy-start) | copy-done | bytes 536
  23.2 0.5 %copy.5 = f32[128]{0:T(128)} copy(f32[128]{0:T(128)S(1)} %bitcast.5) | data formatting | bytes 1024
Async XLA Ops:
  22.6 0.6 %copy-start = (f32[1,128]{1,0:T(1,128)S(1)}, f32[1,128]{1,0:T(1,128)}, u32[]{:S(2)}) copy-start(f32[1,128]{1,0:T(1,128)} %shard_map.37) | copy-start | bytes 1540

commit v2 on v1

--- a/solution.py
+++ b/solution.py
@@ -12,7 +12,7 @@
 MESH = pl.DeviceIdType.MESH
 LANES = 128
 PAIR = 2
-PIECES = 4
+PIECES = 8
 CLASS_STEP = 65536
 EXACT = 2**24
 
@@ -37,6 +37,8 @@
     best_far,
     ret_out,
     ret_in,
+    key_column,
+    entered,
     load_sem,
     send_sem,
     recv_sem,
@@ -84,63 +86,58 @@
     load_rows = pltpu.make_async_copy(emb_hbm, side.at[0], load_sem.at[2])
 
     half = PIECES // 2
-    up = [copy(("up", k), emb_hbm.at[span(k), :], piece(side, 1, k), to_along) for k in range(PIECES)]
-    swing = [
-        copy(("swing", k), emb_hbm.at[span(k), :], piece(side, 3, k), to_column)
-        for k in range(half, PIECES)
-    ]
-    swing_up = [
-        copy(("swing_up", k), piece(side, 3, k), piece(side, 3, k), to_along)
-        for k in range(half, PIECES)
-    ]
+    steps = [(0, 2), (2, 2), (4, 2), (6, 1), (7, 1)]
+    low_steps = steps[:2]
+    high_steps = [(4, 2), (6, 2)]
+
+    def rows_of(step):
+        return emb_hbm.at[span(*step), :]
+
     key_up = [
         copy("label_up", label_hbm, key_side.at[1, 0], to_along),
         copy("rank_up", rank_hbm, key_side.at[1, 1], to_along),
     ]
-    wide = [
-        copy(("wide", k), emb_hbm.at[span(k), :], piece(side, 2, k), to_column)
-        for k in range(PIECES)
-    ]
+    up = [copy(("up", t), rows_of(t), piece(side, 1, *t), to_along) for t in steps]
+    swing = [copy(("swing", t), rows_of(t), piece(side, 3, *t), to_column) for t in high_steps]
+    swing_up = [
+        copy(("swing_up", t), piece(side, 3, *t), piece(side, 3, *t), to_along) for t in high_steps
+    ]
+    wide = copy("wide", emb_hbm, side.at[2], to_column)
     wide_outer = [
-        copy(("wide_outer", k), piece(side, 1, k), piece(side, 3, k), to_column)
-        for k in range(half)
+        copy(("wide_outer", t), piece(side, 1, *t), piece(side, 3, *t), to_column)
+        for t in low_steps
     ]
     key_wide = copy("key_wide", key_side.at[pl.ds(0, 2)], key_side.at[pl.ds(2, 2)], to_column)
     pass_own = copy("pass_own", emb_hbm, twin.at[0], to_twin)
     pass_outer = [
-        copy(("pass_outer", k), piece(side, 1, k), piece(twin, 1, k), to_twin)
-        for k in range(PIECES)
+        copy(("pass_outer", t), piece(side, 1, *t), piece(twin, 1, *t), to_twin) for t in steps
     ]
     key_pass = copy("key_pass", key_side.at[pl.ds(0, 2)], key_twin, to_twin)
-    cross_own = [
-        copy(("cross_own", k), emb_hbm.at[span(k), :], piece(far_rows, 0, k), to_across)
-        for k in range(half, PIECES)
-    ]
+    upper = (half, half)
+    lower = (0, half)
+    cross_own = copy("cross_own", rows_of(upper), piece(far_rows, 0, *upper), to_across)
     cross_outer = [
-        copy(("cross_outer", k), piece(side, 1, k), piece(far_rows, 1, k), to_across)
-        for k in range(PIECES)
+        copy(("cross_outer", t), piece(side, 1, *t), piece(far_rows, 1, *t), to_across)
+        for t in steps
     ]
     key_cross = copy("key_cross", key_side.at[pl.ds(0, 2)], key_far.at[pl.ds(0, 2)], to_across)
-    lend = [
-        copy(("lend", k), emb_hbm.at[span(k), :], relay.at[span(k), :], to_part)
-        for k in range(half)
-    ]
+    lend = [copy(("lend", t), rows_of(t), relay.at[span(*t), :], to_part) for t in low_steps]
     lend_on = [
         copy(
-            ("lend_on", k),
-            relay.at[span(k), :],
-            piece(far_rows, 0, k),
+            ("lend_on", t),
+            relay.at[span(*t), :],
+            piece(far_rows, 0, *t),
             {"parts": 1 - part, "clus": across},
         )
-        for k in range(half)
+        for t in low_steps
     ]
     share_own = [
-        copy(("share_own", k), piece(far_rows, 0, k), piece(far_rows, 2, k), to_twin)
-        for k in range(PIECES)
+        copy(("share_own", t), piece(far_rows, 0, *t), piece(far_rows, 2, *t), to_twin)
+        for t in (lower, upper)
     ]
     share_outer = [
-        copy(("share_outer", k), piece(far_rows, 1, k), piece(far_rows, 3, k), to_twin)
-        for k in range(PIECES)
+        copy(("share_outer", t), piece(far_rows, 1, *t), piece(far_rows, 3, *t), to_twin)
+        for t in steps
     ]
     key_share = copy("key_share", key_far.at[pl.ds(0, 2)], key_far.at[pl.ds(2, 2)], to_twin)
     back = {
@@ -170,15 +167,17 @@
     def cluster(key):
         return jnp.floor(key * (1.0 / CLASS_STEP))
 
-    def column(key_ref, slot):
-        return jnp.transpose(jnp.broadcast_to(key_of(key_ref, slot), (LANES, rows)))
-
-    def visit(source, slot, first, count, key_ref, tiles, far_slot=None):
-        size = count * chunk
-        cand_key = column(key_ref, slot)[first * chunk : first * chunk + size]
+    def columns(first, ref, slots):
+        for n in range(slots):
+            key = jnp.broadcast_to(key_of(ref, n), (LANES, rows))
+            key_column[first + n] = jnp.transpose(key)
+
+    def visit(source, slot, first_key, step, tiles, reversed_too=False):
+        place = span(*step)
+        cand_key = key_column[first_key + slot, place, :]
         cand_cluster = cluster(cand_key)
         members = side[tiles[0] : tiles[-1] + 1].reshape(len(tiles) * rows, side.shape[2])
-        scores = nt_dot(source[slot, span(first, count), :], members)
+        scores = nt_dot(source[slot, place, :], members)
         reverse = None
         for n, tile in enumerate(tiles):
             score = scores[:, n * rows : (n + 1) * rows]
@@ -187,14 +186,19 @@
             earlier = same & (cand_key < member_key)
             top = jnp.max(jnp.where(earlier, score, -1.0), axis=0, keepdims=True)
             best[tile] = jnp.maximum(best[tile], top)
-            if far_slot is not None:
+            if reversed_too:
                 later = jnp.where(same & (cand_key > member_key), score, -1.0)
                 reverse = later if reverse is None else jnp.maximum(reverse, later)
-        if far_slot is not None:
-            part_rows = span(first, count)
-            best_far[far_slot, part_rows, :] = jnp.maximum(
-                best_far[far_slot, part_rows, :], reverse
-            )
+        if reversed_too:
+            best_far[slot, place, :] = jnp.maximum(best_far[slot, place, :], reverse)
+
+    def visit_far(slot, step, tiles):
+        visit(far_rows, slot, 4, step, tiles, True)
+
+    def visit_half(tiles):
+        for slot in range(2):
+            visit(side, slot, 0, whole, tiles)
+            visit(twin, slot, 2, whole, tiles)
 
     def open_inner(gives_here):
         load_label.start()
@@ -203,34 +207,37 @@
         met = greet([to_along, to_across, to_column, to_twin, to_part])
         best[...] = jnp.full(best.shape, -1.0, jnp.float32)
         pl.semaphore_wait(barrier, met)
+        pl.semaphore_signal(entered.at[0], inc=1, device_id=to_column, device_id_type=MESH)
         if gives_here:
-            for c in lend + cross_own:
+            cross_own.start()
+            for c in lend:
                 c.start()
-        for c in wide:
-            c.start()
+        wide.start()
         pass_own.start()
+        pl.semaphore_wait(entered.at[0], 1)
+        pl.semaphore_signal(entered.at[1], inc=1, device_id=to_along, device_id_type=MESH)
         load_label.wait()
         load_rank.wait()
-        for c in key_up:
-            c.wait_recv()
+        settle(key_up)
+        if gives_here:
+            key_cross.start()
         key_pass.start()
         key_wide.start()
+
+    def outer_arrived(n, gives_here):
+        up[n].wait_recv()
         if gives_here:
-            key_cross.start()
-
-    def outer_arrived(k, gives_here):
-        up[k].wait_recv()
-        if gives_here:
-            cross_outer[k].start()
-        if k < half:
-            wide_outer[k].start()
-        pass_outer[k].start()
+            cross_outer[n].start()
+        if n < len(low_steps):
+            wide_outer[n].start()
+        pass_outer[n].start()
 
     def settle(copies):
         for c in copies:
             c.wait_recv()
 
-    inner_sent = wide + wide_outer + pass_outer + [pass_own, key_wide, key_pass]
+    inner_sent = wide_outer + pass_outer + [wide, pass_own, key_wide, key_pass]
+    whole = (0, PIECES)
 
     def result(slots):
         value = ret_in[slots[0]]
@@ -238,18 +245,33 @@
             value = jnp.maximum(value, ret_in[slot])
         return value
 
+    def send_home(slot):
+        ret_out[4 + slot] = jnp.max(jnp.transpose(best_far[slot]), axis=0, keepdims=True)
+        home[slot].start()
+
     near_tiles = [0, 1, 2]
     last_tile = [3]
+    all_tiles = near_tiles + last_tile
+
+    def send_back():
+        for tile, name in ((3, "outer_wide"), (1, "outer"), (2, "inner")):
+            ret_out[tile] = best[tile]
+            back[name].start()
 
     @pl.when(jnp.logical_not(is_inner))
     def _():
-        met = greet([to_along, to_column])
+        met = greet([to_along])
         pl.semaphore_wait(barrier, met)
-        for c in key_up + up + swing:
+        for c in key_up + up:
+            c.start()
+        pl.semaphore_wait(entered.at[1], 1)
+        for c in swing:
             c.start()
         for c, onward in zip(swing, swing_up, strict=True):
             c.wait_recv()
             onward.start()
+        for c in key_up + up + swing + swing_up:
+            c.wait_send()
         back["outer"].wait_recv()
         back["outer_wide"].wait_recv()
 
@@ -263,92 +285,82 @@
         def _():
             out_ref[...] = result([0, 1])
 
-        for c in key_up + up + swing + swing_up:
-            c.wait_send()
-
     @pl.when(is_inner & gives)
     def _():
         open_inner(True)
-        for k in range(PIECES):
-            outer_arrived(k, True)
+        for n in range(len(steps)):
+            outer_arrived(n, True)
         load_rows.wait()
-        settle([key_wide, key_pass, pass_own] + pass_outer + wide)
-        for slot in range(2):
-            visit(side, slot, 0, PIECES, key_side, near_tiles)
-            visit(twin, slot, 0, PIECES, key_twin, near_tiles)
-        for tile in near_tiles[1:]:
-            ret_out[tile] = best[tile]
-        back["outer"].start()
-        back["inner"].start()
+        settle([key_wide, key_pass, pass_own, wide] + pass_outer)
+        columns(0, key_side, 2)
+        columns(2, key_twin, 2)
         settle(wide_outer + swing_up)
-        for slot in range(2):
-            visit(side, slot, 0, PIECES, key_side, last_tile)
-            visit(twin, slot, 0, PIECES, key_twin, last_tile)
-        ret_out[3] = best[3]
-        back["outer_wide"].start()
+        visit_half(all_tiles)
+        send_back()
+        for c in inner_sent + lend + cross_outer + [cross_own, key_cross]:
+            c.wait_send()
         back["inner"].wait_recv()
         home[0].wait_recv()
         home[2].wait_recv()
         out_ref[...] = jnp.maximum(best[0], result([1, 2, 3]))
-        for c in inner_sent + lend + cross_own + cross_outer + [key_cross] + list(back.values()):
+        for c in back.values():
             c.wait_send()
 
     @pl.when(is_inner & jnp.logical_not(gives))
     def _():
         best_far[...] = jnp.full(best_far.shape, -1.0, jnp.float32)
         open_inner(False)
-        for k in range(half):
-            outer_arrived(k, False)
-            lend[k].wait_recv()
-            lend_on[k].start()
-            cross_own[k].wait_recv()
-            share_own[half + k].start()
+        for n in range(2):
+            outer_arrived(n, False)
+            lend[n].wait_recv()
+            lend_on[n].start()
+        cross_own.wait_recv()
+        share_own[1].start()
         outer_arrived(2, False)
-        key_cross.wait_recv()
+        settle([key_cross])
         key_share.start()
         cross_outer[0].wait_recv()
         share_outer[0].start()
         outer_arrived(3, False)
+        outer_arrived(4, False)
         cross_outer[1].wait_recv()
         share_outer[1].start()
         load_rows.wait()
-        settle([key_wide, key_pass, pass_own] + pass_outer + wide)
-        for slot in range(2):
-            visit(side, slot, 0, PIECES, key_side, near_tiles)
-            visit(twin, slot, 0, PIECES, key_twin, near_tiles)
-        for k in range(half):
-            lend_on[k].wait_recv()
-            share_own[k].start()
+        settle([key_wide, key_pass, pass_own, wide] + pass_outer)
+        columns(0, key_side, 2)
+        columns(2, key_twin, 2)
+        visit_half(near_tiles)
+        settle(lend_on)
+        share_own[0].start()
         cross_outer[2].wait_recv()
         share_outer[2].start()
-        key_share.wait_recv()
-        visit(far_rows, 0, 0, PIECES, key_far, near_tiles, 0)
+        settle([key_share])
+        columns(4, key_far, 4)
+        visit_far(0, whole, near_tiles)
         settle(share_own)
-        visit(far_rows, 2, 0, PIECES, key_far, near_tiles, 2)
+        visit_far(2, whole, near_tiles)
         cross_outer[3].wait_recv()
         share_outer[3].start()
-        visit(far_rows, 1, 0, PIECES, key_far, near_tiles, 1)
         settle(wide_outer + swing_up)
-        for slot in range(2):
-            visit(side, slot, 0, PIECES, key_side, last_tile)
-            visit(twin, slot, 0, PIECES, key_twin, last_tile)
+        visit_half(last_tile)
+        visit_far(0, whole, last_tile)
+        visit_far(2, whole, last_tile)
+        cross_outer[4].wait_recv()
+        share_outer[4].start()
+        visit_far(1, whole, all_tiles)
+        settle(share_outer[:3])
+        visit_far(3, (0, 6), all_tiles)
         for slot in range(3):
-            visit(far_rows, slot, 0, PIECES, key_far, last_tile, slot)
-        for slot in range(3):
-            ret_out[4 + slot] = jnp.max(jnp.transpose(best_far[slot]), axis=0, keepdims=True)
-        for c in home[:3]:
-            c.start()
-        settle(share_outer)
-        visit(far_rows, 3, 0, PIECES, key_far, near_tiles + last_tile, 3)
-        for tile in near_tiles[1:] + last_tile:
-            ret_out[tile] = best[tile]
-        for c in back.values():
-            c.start()
-        ret_out[7] = jnp.max(jnp.transpose(best_far[3]), axis=0, keepdims=True)
-        home[3].start()
+            send_home(slot)
+        settle(share_outer[3:])
+        visit_far(3, (6, 2), all_tiles)
+        send_back()
+        send_home(3)
+        for c in inner_sent + lend_on + share_own + share_outer + [key_share]:
+            c.wait_send()
         back["inner"].wait_recv()
         out_ref[...] = jnp.maximum(best[0], result([1]))
-        for c in inner_sent + lend_on + share_own + share_outer + [key_share] + home + list(back.values()):
+        for c in home + list(back.values()):
             c.wait_send()
 
 
@@ -362,7 +374,7 @@
     kept = embeddings.dtype
     out = pl.pallas_call(
         dedup_kernel,
-        out_shape=jax.ShapeDtypeStruct((1, rows), jnp.float32),
+        out_shape=pltpu.VMEM((1, rows), jnp.float32),
         in_specs=[pl.BlockSpec(memory_space=pl.ANY)] * 3,
         out_specs=pl.BlockSpec(memory_space=pltpu.VMEM),
         scratch_shapes=[
@@ -377,6 +389,8 @@
             pltpu.VMEM((4, rows, rows), jnp.float32),
             pltpu.VMEM((8, 1, rows), jnp.float32),
             pltpu.VMEM((4, 1, rows), jnp.float32),
+            pltpu.VMEM((8, rows, rows), jnp.float32),
+            pltpu.SemaphoreType.REGULAR((2,)),
             dma((3,)),
             dma((COPIES,)),
             dma((COPIES,)),

time: 23.9 us -> 23.1 us (0.967)
  local copies, waits for them, and re-layouts: 1.1 us -> 0.51 us
    unnamed x3 -> x1, local copies, waits for them, and re-layouts: 1.1 us -> 0.51 us
where the time goes in v2:
time: 23.1 us; the launch traced here: 23 us
  Pallas kernels  22.4 us (97%)
  local copies, waits for them, and re-layouts  0.51 us (2%)
    pallas_call x1, Pallas kernels, kernel_body(): pl.pallas_call(dedup_kernel, out_shape=pltpu.VMEM((1, rows), jnp.float32)...  22.4 us
    unnamed x1, local copies, waits for them, and re-layouts  0.51 us

profile of v2, /device:TPU:0, one launch (start us, length us, event | category | flops | bytes accessed | tf_op | source)
XLA Modules:
  0.0 23.0 jit_solution(4525200372868252874)
XLA Ops:
  0.0 22.4 %shard_map.37 = f32[1,128]{1,0:T(1,128)S(1)} custom-call(bf16[128,1024]{1,0:T(8,128)(2,1)} %emb_hbm.1, s32[1,128]{1,0:T(1,128)} %bitcast.4, s32[1,128]{1,0:T(1,128)} %bitcast.5), custom_call_target="tpu_custom_call" | custom-call | tf_op jit(solution)/shard_map/pallas_call | solution.py:375
  22.5 0.5 %copy.5 = f32[128]{0:T(128)} copy(f32[128]{0:T(128)S(1)} %bitcast.3) | data formatting | bytes 1024

commit v3 on v2

--- a/solution.py
+++ b/solution.py
@@ -195,10 +195,21 @@
     def visit_far(slot, step, tiles):
         visit(far_rows, slot, 4, step, tiles, True)
 
+    def visit_one(source, first_key, tiles):
+        width = side.shape[2]
+        cand_key = key_column[first_key : first_key + 2].reshape(2 * rows, rows)
+        cand_cluster = cluster(cand_key)
+        members = side[tiles[0] : tiles[-1] + 1].reshape(len(tiles) * rows, width)
+        scores = nt_dot(source[0:2].reshape(2 * rows, width), members)
+        for n, tile in enumerate(tiles):
+            member_key = key_of(key_side, tile)
+            earlier = (cand_cluster == cluster(member_key)) & (cand_key < member_key)
+            score = jnp.where(earlier, scores[:, n * rows : (n + 1) * rows], -1.0)
+            best[tile] = jnp.maximum(best[tile], jnp.max(score, axis=0, keepdims=True))
+
     def visit_half(tiles):
-        for slot in range(2):
-            visit(side, slot, 0, whole, tiles)
-            visit(twin, slot, 2, whole, tiles)
+        visit_one(side, 0, tiles)
+        visit_one(twin, 2, tiles)
 
     def open_inner(gives_here):
         load_label.start()
@@ -310,52 +321,54 @@
     def _():
         best_far[...] = jnp.full(best_far.shape, -1.0, jnp.float32)
         open_inner(False)
+        columns(0, key_side, 2)
+        load_rows.wait()
         for n in range(2):
             outer_arrived(n, False)
             lend[n].wait_recv()
             lend_on[n].start()
         cross_own.wait_recv()
         share_own[1].start()
-        outer_arrived(2, False)
         settle([key_cross])
         key_share.start()
+        outer_arrived(2, False)
         cross_outer[0].wait_recv()
         share_outer[0].start()
         outer_arrived(3, False)
         outer_arrived(4, False)
+        visit_one(side, 0, [0, 1])
         cross_outer[1].wait_recv()
         share_outer[1].start()
-        load_rows.wait()
-        settle([key_wide, key_pass, pass_own, wide] + pass_outer)
-        columns(0, key_side, 2)
+        settle([key_pass, pass_own] + pass_outer)
         columns(2, key_twin, 2)
-        visit_half(near_tiles)
+        visit_one(twin, 2, [0, 1])
         settle(lend_on)
         share_own[0].start()
+        settle([key_wide, wide])
+        visit_half([2])
         cross_outer[2].wait_recv()
         share_outer[2].start()
         settle([key_share])
         columns(4, key_far, 4)
         visit_far(0, whole, near_tiles)
+        cross_outer[3].wait_recv()
+        share_outer[3].start()
         settle(share_own)
         visit_far(2, whole, near_tiles)
-        cross_outer[3].wait_recv()
-        share_outer[3].start()
+        cross_outer[4].wait_recv()
+        share_outer[4].start()
         settle(wide_outer + swing_up)
         visit_half(last_tile)
         visit_far(0, whole, last_tile)
         visit_far(2, whole, last_tile)
-        cross_outer[4].wait_recv()
-        share_outer[4].start()
         visit_far(1, whole, all_tiles)
         settle(share_outer[:3])
         visit_far(3, (0, 6), all_tiles)
-        for slot in range(3):
-            send_home(slot)
         settle(share_outer[3:])
         visit_far(3, (6, 2), all_tiles)
         send_back()
-        send_home(3)
+        for slot in (1, 3, 0, 2):
+            send_home(slot)
         for c in inner_sent + lend_on + share_own + share_outer + [key_share]:
             c.wait_send()
         back["inner"].wait_recv()

time: 23.1 us -> 22.2 us (0.961)
  Pallas kernels: 22.4 us -> 21.6 us
    pallas_call x1, Pallas kernels: 22.4 us -> 21.6 us  [kernel_body(): pl.pallas_call(dedup_kernel, out_shape=pltpu.VMEM((1, rows), jnp.float32)...]
where the time goes in v3:
time: 22.2 us; the launch traced here: 22.1 us
  Pallas kernels  21.6 us (97%)
  local copies, waits for them, and re-layouts  0.51 us (2%)
    pallas_call x1, Pallas kernels, kernel_body(): pl.pallas_call(dedup_kernel, out_shape=pltpu.VMEM((1, rows), jnp.float32)...  21.6 us
    unnamed x1, local copies, waits for them, and re-layouts  0.51 us

profile of v3, /device:TPU:0, one launch (start us, length us, event | category | flops | bytes accessed | tf_op | source)
XLA Modules:
  0.0 22.1 jit_solution(16764107414240823632)
XLA Ops:
  0.0 21.6 %shard_map.37 = f32[1,128]{1,0:T(1,128)S(1)} custom-call(bf16[128,1024]{1,0:T(8,128)(2,1)} %emb_hbm.1, s32[1,128]{1,0:T(1,128)} %bitcast.4, s32[1,128]{1,0:T(1,128)} %bitcast.5), custom_call_target="tpu_custom_call" | custom-call | tf_op jit(solution)/shard_map/pallas_call | solution.py:388
  21.6 0.5 %copy.5 = f32[128]{0:T(128)} copy(f32[128]{0:T(128)S(1)} %bitcast.3) | data formatting | bytes 1024
